TPU v7x, 128 devices: a whole 4x4x4 slice. The times are simulated.
128 devices in a mesh: dp: 16 (over x, y), tensor: 8 (over z, core).
Axes of the slice: x: 4, y: 4, z: 4, core: 2. Of those that a mesh axis runs over, the one named last changes fastest.
Arguments:
- kv_part: bfloat16 [8, 4096, 12288], P('tensor', 'dp'), may hold values from -2 to 2
- queries: bfloat16 [8192, 6144], P('dp', 'tensor'), may hold values from -6 to 6
- w_out: bfloat16 [6144, 8192], P('tensor'), may hold values from -0.078125 to 0.078125
- d_out: bfloat16 [8192, 8192], P('dp', 'tensor'), may hold values from -48 to 48
- nbr_owner: int32 [128, 2], replicated, may hold values from 0 to 15, as said below
- nbr_slot: int32 [128, 2], replicated, may hold values from 0 to 1, as said below
Outputs:
- mixed: bfloat16 [8192, 8192], P('dp', 'tensor')
- d_kv: bfloat16 [4096, 12288], P('dp', 'tensor')
Inputs may be any that keep to these rules, and one draw needn't show every extreme that they name: `nbr_owner`: the two neighbours of one span have different owners. `nbr_slot`: all neighbours that the spans of one dp index r (spans r * 8 to (r + 1) * 8 - 1) take from one owner have the same slot.
All inputs are finite; a program needn't handle non-finite values.
Results may differ from a plain program's by a relative error of at most 0.025.
Values may be sent and summed in bfloat16 or wider, within the bound.
A program may use at most 192 MiB of HBM per device.

v0:
```python
import jax
import jax.numpy as jnp
from jax import lax
from jax.sharding import PartitionSpec as P

HD = 128
SPAN = 64
NBR_LEN = 128
NB_DEV = 2


def local(kv_part, queries, w_out, d_out, nbr_owner, nbr_slot):
    dp_count = lax.axis_size("dp")
    reader = lax.axis_index("dp")
    head_width = w_out.shape[0]
    heads_here = head_width // HD
    share_width = 2 * head_width
    span_count = queries.shape[0] // SPAN
    read_count = 2 * span_count
    block_width = NBR_LEN * share_width
    local_partial = kv_part[0]
    summed = lax.psum(local_partial, "tensor").astype(jnp.float32)
    shares = lax.dynamic_slice_in_dim(
        summed, lax.axis_index("tensor") * share_width, share_width, 1
    ).astype(jnp.bfloat16)
    share_blocks = shares.reshape(NB_DEV, block_width)
    owner_ids = jnp.arange(dp_count, dtype=jnp.int32)
    slot_ids = jnp.arange(NB_DEV, dtype=jnp.int32)
    owner_hits = nbr_owner[:, :, None] == owner_ids[None, None, :]
    per_reader = owner_hits.reshape(dp_count, read_count, dp_count)
    reads_from = jnp.any(per_reader, axis=1)
    slot_from = jnp.max(jnp.where(per_reader, nbr_slot.reshape(dp_count, read_count, 1), 0), axis=1)
    my_owner = lax.dynamic_slice_in_dim(nbr_owner, reader * span_count, span_count, 0).reshape(
        read_count
    )
    my_slot = lax.dynamic_slice_in_dim(nbr_slot, reader * span_count, span_count, 0).reshape(
        read_count
    )
    read_table = (my_owner[:, None] == owner_ids[None, :]).astype(jnp.bfloat16)
    serving = lax.dynamic_index_in_dim(reads_from, reader, 1, False)
    serving_slot = lax.dynamic_index_in_dim(slot_from, reader, 1, False)
    owner_select = ((serving_slot[:, None] == slot_ids[None, :]) & serving[:, None]).astype(
        jnp.bfloat16
    )
    everyone = lax.all_gather(share_blocks, "dp", axis=0, tiled=True)
    wanted = (my_owner * NB_DEV + my_slot)[:, None] == jnp.arange(
        dp_count * NB_DEV, dtype=jnp.int32
    )[None, :]
    neighbours = jnp.dot(
        wanted.astype(jnp.bfloat16), everyone, preferred_element_type=jnp.float32
    ).astype(jnp.bfloat16)
    layout = neighbours.reshape(span_count, 2 * NBR_LEN, heads_here, 2, HD)
    keys = layout[:, :, :, 0]
    values = layout[:, :, :, 1]
    query_view = queries.reshape(span_count, SPAN, heads_here, HD)
    factor = HD ** (-0.5)
    scores = (
        jnp.einsum("cqhd,ckhd->chqk", query_view, keys, preferred_element_type=jnp.float32) * factor
    )
    highest = jnp.max(scores, axis=-1, keepdims=True)
    expo = jnp.exp(scores - highest)
    probs = expo / jnp.sum(expo, axis=-1, keepdims=True)
    probs_low = probs.astype(jnp.bfloat16)
    attended = jnp.einsum("chqk,ckhd->cqhd", probs_low, values, preferred_element_type=jnp.float32)
    attended = attended.astype(jnp.bfloat16).reshape(span_count * SPAN, head_width)
    partial_out = jnp.dot(attended, w_out, preferred_element_type=jnp.float32)
    mixed = lax.psum_scatter(
        partial_out.astype(jnp.bfloat16), "tensor", scatter_dimension=1, tiled=True
    )
    grad_attended = lax.dot_general(
        lax.all_gather(d_out, "tensor", axis=1, tiled=True),
        w_out,
        (((1,), (1,)), ((), ())),
        preferred_element_type=jnp.float32,
    ).astype(jnp.bfloat16)
    grad_view = grad_attended.reshape(span_count, SPAN, heads_here, HD)
    grad_values = jnp.einsum(
        "chqk,cqhd->ckhd", probs_low, grad_view, preferred_element_type=jnp.float32
    )
    grad_probs = jnp.einsum(
        "cqhd,ckhd->chqk", grad_view, values, preferred_element_type=jnp.float32
    )
    grad_scores = probs * (grad_probs - jnp.sum(probs * grad_probs, axis=-1, keepdims=True))
    grad_scores = grad_scores.astype(jnp.bfloat16)
    grad_keys = (
        jnp.einsum("chqk,cqhd->ckhd", grad_scores, query_view, preferred_element_type=jnp.float32)
        * factor
    )
    grad_blocks = jnp.stack([grad_keys, grad_values], axis=3).reshape(read_count, block_width)
    per_owner = lax.dot_general(
        read_table.astype(jnp.float32),
        grad_blocks,
        (((0,), (0,)), ((), ())),
        precision=lax.Precision.HIGHEST,
        preferred_element_type=jnp.float32,
    ).astype(jnp.bfloat16)
    returned = lax.all_to_all(per_owner, "dp", split_axis=0, concat_axis=0, tiled=True)
    owner_grad = lax.dot_general(
        owner_select, returned, (((0,), (0,)), ((), ())), preferred_element_type=jnp.float32
    )
    d_kv = owner_grad.astype(jnp.bfloat16).reshape(NB_DEV * NBR_LEN, share_width)
    return (mixed, d_kv)


def solution(mesh):
    placed = (
        P("tensor", "dp", None),
        P("dp", "tensor"),
        P("tensor", None),
        P("dp", "tensor"),
        P(),
        P(),
    )
    return jax.shard_map(
        local,
        mesh=mesh,
        in_specs=placed,
        out_specs=(P("dp", "tensor"), P("dp", "tensor")),
        check_vma=False,
    )
```

profile of v0, /device:TPU:28, one launch (start us, length us, event | category | flops | bytes accessed | tf_op | source)
XLA Modules:
  0.0 541.4 jit_solution(5792027820581872935)
XLA Ops:
  8.0 89.0 %all-reduce.2.cloned.1.call-done = bf16[256,12288]{1,0:T(8,128)(2,1)} async-done(((bf16[256,12288]{1,0:T(8,128)(2,1)}), bf16[256,12288]{1,0:T(8,128)(2,1)}) %all-reduce.2.cloned.1.call-update) | async-done | bytes 6291472 | tf_op jit(solution)/shard_map/psum | solution.py:22
  102.8 85.0 %all-gather.6.cloned.1.call-done = bf16[16,2,196608]{2,1,0:T(2,128)(2,1)} async-done(((bf16[1,2,196608]{2,1,0:T(2,128)(2,1)}), bf16[16,2,196608]{2,1,0:T(2,128)(2,1)}) %all-gather.6.cloned.1.call-update) | async-done | bytes 12582928 | tf_op jit(solution)/shard_map/all_gather | solution.py:45
  187.7 11.3 %reshape.63 = bf16[32,196608]{1,0:T(8,128)(2,1)} reshape(bf16[16,2,196608]{2,1,0:T(2,128)(2,1)} %all-gather.6.cloned.1.call-done) | data formatting | bytes 25165824
  199.0 10.4 %convolution_convert_fusion.1 = bf16[16,196608]{1,0:T(8,128)(2,1)} fusion(bf16[32,196608]{1,0:T(8,128)(2,1)} %reshape.63, s32[16]{0:T(128)S(1)} %multiply_add_fusion), kind=kOutput, calls=%fused_computation.2 | convolution fusion | flops 204472832 | bytes 18874432 | tf_op jit(solution)/shard_map/dot_general | solution.py:49
  209.4 9.9 %reshape.56 = bf16[8,256,6,2,128]{4,3,2,1,0:T(2,128)(2,1)} reshape(bf16[16,196608]{1,0:T(8,128)(2,1)} %convolution_convert_fusion.1) | data formatting | bytes 12582912 | tf_op jit(solution)/shard_map/reshape | solution.py:52
  219.3 13.7 %fusion.42 = (bf16[8,256,6,1,128]{4,3,2,1,0:T(2,128)(2,1)S(1)}, bf16[8,256,6,1,128]{4,3,2,1,0:T(2,128)(2,1)}) fusion(bf16[8,256,6,2,128]{4,3,2,1,0:T(2,128)(2,1)} %reshape.56), kind=kLoop, calls=%fused_computation.54 | loop fusion | bytes 12582912 | tf_op jit(solution)/shard_map/slice | solution.py:53
  234.2 2.3 fusion.43
  236.5 9.2 %fusion.12 = bf16[8,64,6,128]{3,1,2,0:T(8,128)(2,1)} fusion(bf16[8,256,6,1,128]{4,3,2,1,0:T(2,128)(2,1)} %get-tuple-element.3, f32[8,6,64]{2,1,0:T(8,128)S(1)} %get-tuple-element.4, f32[8,6,256,64]{2,3,1,0:T(8,128)S(1)} %fusion.4), kind=kOutput, calls=%fused_computation.27 | convolution fusion | flops 205655296 | bytes 7090176 | tf_op jit(solution)/shard_map/chqk,ckhd->cqhd/dot_general | solution.py:64
  247.4 13.4 %convolution_convert_fusion.3 = bf16[512,8192]{1,0:T(8,128)(2,1)} fusion(bf16[768,8192]{1,0:T(8,128)(2,1)} %param.8, bf16[64,8,6,128]{3,2,1,0:T(8,128)(2,1)S(1)} %bitcast.71), kind=kOutput, calls=%fused_computation.6 | convolution fusion | flops 6446645248 | bytes 21757952 | tf_op jit(solution)/shard_map/dot_general | solution.py:66
  260.9 13.5 %convolution_convert_fusion.5 = bf16[512,768]{1,0:T(8,128)(2,1)} fusion(bf16[512,8192]{1,0:T(8,128)(2,1)} %all-gather.4.cloned.1.call-done, bf16[768,8192]{1,0:T(8,128)(2,1)} %param.8), kind=kOutput, calls=%fused_computation.26 | convolution fusion | flops 6442844160 | bytes 21757952 | tf_op jit(solution)/shard_map/dot_general | solution.py:70
  274.4 2.9 reshape.59
  277.3 10.3 %convolution_bitcast_fusion = f32[8,256,6,1,128]{4,1,2,0,3:T(8,128)} fusion(bf16[8,64,6,128]{3,2,1,0:T(8,128)(2,1)} %reshape.59, f32[8,6,64]{2,1,0:T(8,128)S(1)} %get-tuple-element.4, f32[8,6,256,64]{2,3,1,0:T(8,128)S(1)} %fusion.4), kind=kOutput, calls=%fused_computation.20 | convolution fusion | flops 205262080 | bytes 10235904 | tf_op jit(solution)/shard_map/chqk,cqhd->ckhd/dot_general | solution.py:77
  287.6 7.2 %multiply_reduce_fusion = (f32[8,6,64]{2,1,0:T(8,128)S(1)}, f32[8,6,64,256]{3,2,1,0:T(8,128)}) fusion(f32[8,6,64,256]{3,2,1,0:T(8,128)} %get-tuple-element.5, f32[8,6,64]{2,1,0:T(8,128)S(1)} %get-tuple-element.4, bf16[8,256,6,1,128]{4,3,2,1,0:T(2,128)(2,1)} %get-tuple-element.3, bf16[8,64,6,128]{3,2,1,0:T(8,128)(2,1)} %reshape.59), kind=kOutput, calls=%fused_computation.18 | convolution fusion | flops 203682816 | bytes 10248192 | tf_op jit(solution)/shard_map/cqhd,ckhd->chqk/dot_general | solution.py:80
  294.8 11.7 %multiply_bitcast_fusion = f32[8,256,6,1,128]{4,1,2,0,3:T(8,128)} fusion(f32[8,6,64,256]{3,2,1,0:T(8,128)} %get-tuple-element.7, f32[8,6,64]{2,1,0:T(8,128)S(1)} %get-tuple-element.6, bf16[8,64,6,128]{3,2,1,0:T(8,128)(2,1)} %reshape.57, f32[8,6,64]{2,1,0:T(8,128)S(1)} %get-tuple-element.4, f32[8,6,256,64]{2,3,1,0:T(8,128)S(1)} %fusion.4), kind=kOutput, calls=%fused_computation.9 | convolution fusion | flops 208407808 | bytes 13393920 | tf_op jit(solution)/shard_map/chqk,cqhd->ckhd/dot_general | solution.py:86
  306.5 10.9 %pad_maximum_fusion = f32[8,256,6,2,128]{4,1,2,0,3:T(8,128)} fusion(f32[8,256,6,1,128]{4,1,2,0,3:T(8,128)} %convolution_bitcast_fusion, f32[8,256,6,1,128]{4,1,2,0,3:T(8,128)} %multiply_bitcast_fusion), kind=kLoop, calls=%fused_computation.5 | loop fusion | flops 3145728 | bytes 25165824 | tf_op jit(solution)/shard_map/stack | solution.py:89
  317.4 22.2 %copy.84 = f32[8,256,6,2,128]{4,3,2,1,0:T(2,128)} copy(f32[8,256,6,2,128]{4,1,2,0,3:T(8,128)} %pad_maximum_fusion) | data formatting | bytes 25165824 | tf_op jit(solution)/shard_map/stack | solution.py:89
  339.6 21.3 %reshape.60 = f32[16,196608]{1,0:T(8,128)} reshape(f32[8,256,6,2,128]{4,3,2,1,0:T(2,128)} %copy.84) | data formatting | bytes 25165824 | tf_op jit(solution)/shard_map/reshape | solution.py:89
  360.9 10.9 %fusion.1 = bf16[16,1,196608]{2,0,1:T(8,128)(2,1)} fusion(f32[16,196608]{1,0:T(8,128)} %reshape.60, s32[16]{0:T(128)S(1)} %reshape.53), kind=kOutput, calls=%fused_computation.3 | convolution fusion | flops 607125760 | bytes 18874432 | tf_op jit(solution)/shard_map/dot_general | solution.py:90
  372.3 8.8 %reduce.4 = bf16[16,196608]{1,0:T(8,128)(2,1)} reduce(bf16[16,1,196608]{2,0,1:T(8,128)(2,1)} %fusion.1, bf16[]{:T(256)} %broadcast.20), dimensions={1}, to_apply=%copy.85.reduce_sub_computation | reduce | bytes 12582914 | tf_op jit(solution)/shard_map/all_to_all | solution.py:97
  381.2 9.3 %reshape.67 = bf16[16,2,98304]{2,1,0:T(2,128)(2,1)} reshape(bf16[16,196608]{1,0:T(8,128)(2,1)} %reduce.4) | data formatting | bytes 12582912
  390.5 7.2 %all-to-all-start = ((bf16[16,2,98304]{2,1,0:T(2,128)(2,1)}), bf16[16,2,98304]{2,1,0:T(2,128)(2,1)}, u32[]{:S(2)}, u32[]{:S(2)}) async-start(bf16[16,2,98304]{2,1,0:T(2,128)(2,1)} %reshape.67), calls=%async_computation.1 | async-start | bytes 12582912 | tf_op jit(solution)/shard_map/all_to_all | solution.py:97
  398.8 107.1 %all-to-all-done = bf16[16,2,98304]{2,1,0:T(2,128)(2,1)} async-done(((bf16[16,2,98304]{2,1,0:T(2,128)(2,1)}), bf16[16,2,98304]{2,1,0:T(2,128)(2,1)}, u32[]{:S(2)}, u32[]{:S(2)}) %all-to-all-start) | async-done | bytes 6291488 | tf_op jit(solution)/shard_map/all_to_all | solution.py:97
  505.9 14.3 %reshape.68 = bf16[16,1,196608]{2,1,0:T(2,128)(2,1)} reshape(bf16[16,2,98304]{2,1,0:T(2,128)(2,1)} %all-to-all-done) | data formatting | bytes 12582912
  520.2 12.8 %convolution_convert_fusion.2 = bf16[2,196608]{1,0:T(2,128)(2,1)S(1)} fusion(bf16[16,1,196608]{2,1,0:T(2,128)(2,1)} %reshape.68, s32[16]{0:T(128)S(1)} %dynamic-slice_reduce_fusion, pred[16]{0:T(512)(128)(4,1)S(1)} %dynamic-slice_reduce_fusion.1), kind=kOutput, calls=%fused_computation.4 | convolution fusion | flops 12976192 | bytes 7077968 | tf_op jit(solution)/shard_map/dot_general | solution.py:98
  (39 shorter events, 12.6 us)
Async XLA Ops:
  7.2 89.8 %all-reduce.2.cloned.1.call-start = ((), (), s32[]{:S(2)}) async-start(), calls=%async_computation.2 | async-start | bytes 12582912 | tf_op jit(solution)/shard_map/psum | solution.py:22
  7.9 92.6 %copy-start.2 = (s32[128,2]{0,1:T(2,128)S(1)}, s32[128,2]{0,1:T(2,128)}, u32[]{:S(2)}) copy-start(s32[128,2]{0,1:T(2,128)} %param.11) | copy-start | bytes 3076
  7.9 92.6 %copy-start.3 = (s32[128,2]{0,1:T(2,128)S(1)}, s32[128,2]{0,1:T(2,128)}, u32[]{:S(2)}) copy-start(s32[128,2]{0,1:T(2,128)} %param.10) | copy-start | bytes 3076
  7.9 93.0 %copy-start.1 = (bf16[512,768]{1,0:T(8,128)(2,1)S(1)}, bf16[512,768]{1,0:T(8,128)(2,1)}, u32[]{:S(2)}) copy-start(bf16[512,768]{1,0:T(8,128)(2,1)} %param.7) | copy-start | bytes 2359300
  7.9 179.8 %all-gather.6.cloned.1.call-start = ((), (), s32[]{:S(2)}) async-start(), calls=%async_computation.5 | async-start | bytes 13369344 | tf_op jit(solution)/shard_map/all_gather | solution.py:45
  99.7 161.2 %all-gather.4.cloned.1.call-start = ((), (), s32[]{:S(2)}) async-start(), calls=%async_computation.4 | async-start | bytes 9437184 | tf_op jit(solution)/shard_map/all_gather | solution.py:71
  100.4 434.3 %reduce-scatter.2.cloned.1.call-start = ((), (), s32[]{:S(2)}) async-start(), calls=%async_computation.3 | async-start | bytes 9437184 | tf_op jit(solution)/shard_map/reduce_scatter | solution.py:67
  219.3 13.7 %copy-start = (bf16[8,64,6,128]{3,2,1,0:T(8,128)(2,1)S(1)}, bf16[8,64,6,128]{3,2,1,0:T(8,128)(2,1)}, u32[]{:S(2)}) copy-start(bf16[8,64,6,128]{3,2,1,0:T(8,128)(2,1)} %reshape.57) | copy-start | bytes 2359300
  390.5 115.4 %all-to-all-start = ((bf16[16,2,98304]{2,1,0:T(2,128)(2,1)}), bf16[16,2,98304]{2,1,0:T(2,128)(2,1)}, u32[]{:S(2)}, u32[]{:S(2)}) async-start(bf16[16,2,98304]{2,1,0:T(2,128)(2,1)} %reshape.67), calls=%async_computation.1 | async-start | bytes 12582912 | tf_op jit(solution)/shard_map/all_to_all | solution.py:97
Sparse Core Ops, SparseCore 0:
  10.4 86.5 all-reduce.1
  99.8 87.8 all-gather.5
  189.4 51.1 all-gather.3
  261.0 53.9 reduce-scatter.1
where the time goes:
time: 549 us; the launch traced here: 541 us
  waiting for transfers between devices  283 us (52%)
  local copies, waits for them, and re-layouts  113 us (21%)
  matrix products  101 us (18%)
  other arithmetic  23.6 us (4%)
  between operations  14.1 us (3%)
  starting transfers between devices  7.38 us (1%)
    all_to_all x1, waiting for transfers between devices, local(): lax.all_to_all(per_owner, 'dp', split_axis=0, concat_axis=0, tiled=True)  107 us
    psum x1, waiting for transfers between devices, local(): summed = lax.psum(local_partial, 'tensor').astype(jnp.float32)  89 us
    all_gather x1, waiting for transfers between devices, local(): everyone = lax.all_gather(share_blocks, 'dp', axis=0, tiled=True)  85 us
    unnamed x14, local copies, waits for them, and re-layouts  36.7 us
    another operation x1, local copies, waits for them, and re-layouts, local(): jnp.stack([grad_keys, grad_values], axis=3).reshape(read_count, block_width)  22.2 us
    reshape x1, local copies, waits for them, and re-layouts, local(): jnp.stack([grad_keys, grad_values], axis=3).reshape(read_count, block_width)  21.3 us
    slice x1, local copies, waits for them, and re-layouts, local(): keys = layout[:, :, :, 0]  13.7 us
    dot_general x1, matrix products, local(): lax.dot_general(lax.all_gather(d_out, 'tensor', axis=1, tiled=True), w_ou...  13.5 us
  transfers between devices with their start and end apart: 5, of which 3 were waited for; matrix products, arithmetic and copies ran while one was open for 43% of the time, Pallas kernels for 0%

commit v1 on v0

--- a/solution.py
+++ b/solution.py
@@ -19,7 +19,7 @@
     read_count = 2 * span_count
     block_width = NBR_LEN * share_width
     local_partial = kv_part[0]
-    summed = lax.psum(local_partial, "tensor").astype(jnp.float32)
+    summed = jnp.sum(lax.all_gather(local_partial, "tensor"), axis=0).astype(jnp.float32)
     shares = lax.dynamic_slice_in_dim(
         summed, lax.axis_index("tensor") * share_width, share_width, 1
     ).astype(jnp.bfloat16)

time: 549 us -> 712 us (1.30)
  waiting for transfers between devices: 283 us -> 425 us
  other arithmetic: 23.6 us -> 43.6 us
    all_gather x0 -> x1, waiting for transfers between devices: none -> 231 us  [local(): lax.all_gather(local_partial, 'tensor')]
    psum x1 -> x0, waiting for transfers between devices: 89 us -> none  [local(): summed = lax.psum(local_partial, 'tensor').astype(jnp.float32)]
    reduce_sum x0 -> x1, other arithmetic: none -> 20 us  [local(): jnp.sum(lax.all_gather(local_partial, 'tensor'), axis=0).astype(jnp.float32)]
  transfers between devices with their start and end apart: 5 -> 5, of which waited for: 3 -> 3; matrix products, arithmetic and copies ran while one was open for 43% -> 33% of each run, Pallas kernels for 0% -> 0%
where the time goes in v1:
time: 712 us; the launch traced here: 704 us
  waiting for transfers between devices  425 us (60%)
  local copies, waits for them, and re-layouts  113 us (16%)
  matrix products  101 us (14%)
  other arithmetic  43.6 us (6%)
  between operations  14.1 us (2%)
  starting transfers between devices  7.4 us (1%)
    all_gather x1, waiting for transfers between devices, local(): lax.all_gather(local_partial, 'tensor')  231 us
    all_to_all x1, waiting for transfers between devices, local(): lax.all_to_all(per_owner, 'dp', split_axis=0, concat_axis=0, tiled=True)  107 us
    all_gather x1, waiting for transfers between devices, local(): everyone = lax.all_gather(share_blocks, 'dp', axis=0, tiled=True)  84.9 us
    unnamed x14, local copies, waits for them, and re-layouts  36.7 us
    another operation x1, local copies, waits for them, and re-layouts, local(): jnp.stack([grad_keys, grad_values], axis=3).reshape(read_count, block_width)  22.2 us
    reshape x1, local copies, waits for them, and re-layouts, local(): jnp.stack([grad_keys, grad_values], axis=3).reshape(read_count, block_width)  21.3 us
    reduce_sum x1, other arithmetic, local(): jnp.sum(lax.all_gather(local_partial, 'tensor'), axis=0).astype(jnp.float32)  20 us
  transfers between devices with their start and end apart: 5, of which 3 were waited for; matrix products, arithmetic and copies ran while one was open for 33% of the time, Pallas kernels for 0%

profile of v1, /device:TPU:28, one launch (start us, length us, event | category | flops | bytes accessed | tf_op | source)
XLA Modules:
  0.0 703.6 jit_solution(5656104867991589531)
XLA Ops:
  7.9 231.2 %all-gather.5.cloned.1.call-done = bf16[8,256,12288]{2,1,0:T(8,128)(2,1)} async-done(((bf16[1,256,12288]{2,1,0:T(8,128)(2,1)}), bf16[8,256,12288]{2,1,0:T(8,128)(2,1)}) %all-gather.5.cloned.1.call-update) | async-done | bytes 50331664 | tf_op jit(solution)/shard_map/all_gather | solution.py:22
  239.1 20.0 %reduce_sum.30 = bf16[256,12288]{1,0:T(8,128)(2,1)} reduce(bf16[8,256,12288]{2,1,0:T(8,128)(2,1)} %all-gather.5.cloned.1.call-done, bf16[]{:T(256)} %constant.11.clone.1), dimensions={0}, to_apply=%region_0.0 | reduce | flops 22020096 | bytes 56623104 | tf_op jit(solution)/shard_map/reduce_sum | solution.py:22
  265.0 84.9 %all-gather.9.cloned.1.call-done = bf16[16,2,196608]{2,1,0:T(2,128)(2,1)} async-done(((bf16[1,2,196608]{2,1,0:T(2,128)(2,1)}), bf16[16,2,196608]{2,1,0:T(2,128)(2,1)}) %all-gather.9.cloned.1.call-update) | async-done | bytes 12582928 | tf_op jit(solution)/shard_map/all_gather | solution.py:45
  349.9 11.3 %reshape.63 = bf16[32,196608]{1,0:T(8,128)(2,1)} reshape(bf16[16,2,196608]{2,1,0:T(2,128)(2,1)} %all-gather.9.cloned.1.call-done) | data formatting | bytes 25165824
  361.2 10.4 %convolution_convert_fusion.1 = bf16[16,196608]{1,0:T(8,128)(2,1)} fusion(bf16[32,196608]{1,0:T(8,128)(2,1)} %reshape.63, s32[16]{0:T(128)S(1)} %multiply_add_fusion), kind=kOutput, calls=%fused_computation.2 | convolution fusion | flops 204472832 | bytes 18874432 | tf_op jit(solution)/shard_map/dot_general | solution.py:49
  371.6 9.9 %reshape.56 = bf16[8,256,6,2,128]{4,3,2,1,0:T(2,128)(2,1)} reshape(bf16[16,196608]{1,0:T(8,128)(2,1)} %convolution_convert_fusion.1) | data formatting | bytes 12582912 | tf_op jit(solution)/shard_map/reshape | solution.py:52
  381.5 13.7 %fusion.42 = (bf16[8,256,6,1,128]{4,3,2,1,0:T(2,128)(2,1)S(1)}, bf16[8,256,6,1,128]{4,3,2,1,0:T(2,128)(2,1)}) fusion(bf16[8,256,6,2,128]{4,3,2,1,0:T(2,128)(2,1)} %reshape.56), kind=kLoop, calls=%fused_computation.54 | loop fusion | bytes 12582912 | tf_op jit(solution)/shard_map/slice | solution.py:53
  398.7 9.2 %fusion.12 = bf16[8,64,6,128]{3,1,2,0:T(8,128)(2,1)} fusion(bf16[8,256,6,1,128]{4,3,2,1,0:T(2,128)(2,1)} %get-tuple-element.3, f32[8,6,64]{2,1,0:T(8,128)S(1)} %get-tuple-element.4, f32[8,6,256,64]{2,3,1,0:T(8,128)S(1)} %fusion.4), kind=kOutput, calls=%fused_computation.27 | convolution fusion | flops 205655296 | bytes 7090176 | tf_op jit(solution)/shard_map/chqk,ckhd->cqhd/dot_general | solution.py:64
  409.6 13.4 %convolution_convert_fusion.3 = bf16[512,8192]{1,0:T(8,128)(2,1)} fusion(bf16[768,8192]{1,0:T(8,128)(2,1)} %param.8, bf16[64,8,6,128]{3,2,1,0:T(8,128)(2,1)S(1)} %bitcast.69), kind=kOutput, calls=%fused_computation.6 | convolution fusion | flops 6446645248 | bytes 21757952 | tf_op jit(solution)/shard_map/dot_general | solution.py:66
  423.1 13.5 %convolution_convert_fusion.5 = bf16[512,768]{1,0:T(8,128)(2,1)} fusion(bf16[512,8192]{1,0:T(8,128)(2,1)} %all-gather.7.cloned.1.call-done, bf16[768,8192]{1,0:T(8,128)(2,1)} %param.8), kind=kOutput, calls=%fused_computation.26 | convolution fusion | flops 6442844160 | bytes 21757952 | tf_op jit(solution)/shard_map/dot_general | solution.py:70
  436.6 2.9 reshape.59
  439.5 10.3 %convolution_bitcast_fusion = f32[8,256,6,1,128]{4,1,2,0,3:T(8,128)} fusion(bf16[8,64,6,128]{3,2,1,0:T(8,128)(2,1)} %reshape.59, f32[8,6,64]{2,1,0:T(8,128)S(1)} %get-tuple-element.4, f32[8,6,256,64]{2,3,1,0:T(8,128)S(1)} %fusion.4), kind=kOutput, calls=%fused_computation.20 | convolution fusion | flops 205262080 | bytes 10235904 | tf_op jit(solution)/shard_map/chqk,cqhd->ckhd/dot_general | solution.py:77
  449.8 7.2 %multiply_reduce_fusion = (f32[8,6,64]{2,1,0:T(8,128)S(1)}, f32[8,6,64,256]{3,2,1,0:T(8,128)}) fusion(f32[8,6,64,256]{3,2,1,0:T(8,128)} %get-tuple-element.5, f32[8,6,64]{2,1,0:T(8,128)S(1)} %get-tuple-element.4, bf16[8,256,6,1,128]{4,3,2,1,0:T(2,128)(2,1)} %get-tuple-element.3, bf16[8,64,6,128]{3,2,1,0:T(8,128)(2,1)} %reshape.59), kind=kOutput, calls=%fused_computation.18 | convolution fusion | flops 203682816 | bytes 10248192 | tf_op jit(solution)/shard_map/cqhd,ckhd->chqk/dot_general | solution.py:80
  457.0 11.7 %multiply_bitcast_fusion = f32[8,256,6,1,128]{4,1,2,0,3:T(8,128)} fusion(f32[8,6,64,256]{3,2,1,0:T(8,128)} %get-tuple-element.7, f32[8,6,64]{2,1,0:T(8,128)S(1)} %get-tuple-element.6, bf16[8,64,6,128]{3,2,1,0:T(8,128)(2,1)} %reshape.57, f32[8,6,64]{2,1,0:T(8,128)S(1)} %get-tuple-element.4, f32[8,6,256,64]{2,3,1,0:T(8,128)S(1)} %fusion.4), kind=kOutput, calls=%fused_computation.9 | convolution fusion | flops 208407808 | bytes 13393920 | tf_op jit(solution)/shard_map/chqk,cqhd->ckhd/dot_general | solution.py:86
  468.7 10.9 %pad_maximum_fusion = f32[8,256,6,2,128]{4,1,2,0,3:T(8,128)} fusion(f32[8,256,6,1,128]{4,1,2,0,3:T(8,128)} %convolution_bitcast_fusion, f32[8,256,6,1,128]{4,1,2,0,3:T(8,128)} %multiply_bitcast_fusion), kind=kLoop, calls=%fused_computation.5 | loop fusion | flops 3145728 | bytes 25165824 | tf_op jit(solution)/shard_map/stack | solution.py:89
  479.6 22.2 %copy.84 = f32[8,256,6,2,128]{4,3,2,1,0:T(2,128)} copy(f32[8,256,6,2,128]{4,1,2,0,3:T(8,128)} %pad_maximum_fusion) | data formatting | bytes 25165824 | tf_op jit(solution)/shard_map/stack | solution.py:89
  501.8 21.3 %reshape.60 = f32[16,196608]{1,0:T(8,128)} reshape(f32[8,256,6,2,128]{4,3,2,1,0:T(2,128)} %copy.84) | data formatting | bytes 25165824 | tf_op jit(solution)/shard_map/reshape | solution.py:89
  523.1 10.9 %fusion.1 = bf16[16,1,196608]{2,0,1:T(8,128)(2,1)} fusion(f32[16,196608]{1,0:T(8,128)} %reshape.60, s32[16]{0:T(128)S(1)} %reshape.53), kind=kOutput, calls=%fused_computation.3 | convolution fusion | flops 607125760 | bytes 18874432 | tf_op jit(solution)/shard_map/dot_general | solution.py:90
  534.5 8.8 %reduce.5 = bf16[16,196608]{1,0:T(8,128)(2,1)} reduce(bf16[16,1,196608]{2,0,1:T(8,128)(2,1)} %fusion.1, bf16[]{:T(256)} %broadcast.20), dimensions={1}, to_apply=%copy.85.reduce_sub_computation | reduce | bytes 12582914 | tf_op jit(solution)/shard_map/all_to_all | solution.py:97
  543.4 9.3 %reshape.67 = bf16[16,2,98304]{2,1,0:T(2,128)(2,1)} reshape(bf16[16,196608]{1,0:T(8,128)(2,1)} %reduce.5) | data formatting | bytes 12582912
  552.7 7.2 %all-to-all-start = ((bf16[16,2,98304]{2,1,0:T(2,128)(2,1)}), bf16[16,2,98304]{2,1,0:T(2,128)(2,1)}, u32[]{:S(2)}, u32[]{:S(2)}) async-start(bf16[16,2,98304]{2,1,0:T(2,128)(2,1)} %reshape.67), calls=%async_computation.1 | async-start | bytes 12582912 | tf_op jit(solution)/shard_map/all_to_all | solution.py:97
  561.0 107.1 %all-to-all-done = bf16[16,2,98304]{2,1,0:T(2,128)(2,1)} async-done(((bf16[16,2,98304]{2,1,0:T(2,128)(2,1)}), bf16[16,2,98304]{2,1,0:T(2,128)(2,1)}, u32[]{:S(2)}, u32[]{:S(2)}) %all-to-all-start) | async-done | bytes 6291488 | tf_op jit(solution)/shard_map/all_to_all | solution.py:97
  668.1 14.3 %reshape.68 = bf16[16,1,196608]{2,1,0:T(2,128)(2,1)} reshape(bf16[16,2,98304]{2,1,0:T(2,128)(2,1)} %all-to-all-done) | data formatting | bytes 12582912
  682.4 12.8 %convolution_convert_fusion.2 = bf16[2,196608]{1,0:T(2,128)(2,1)S(1)} fusion(bf16[16,1,196608]{2,1,0:T(2,128)(2,1)} %reshape.68, s32[16]{0:T(128)S(1)} %dynamic-slice_reduce_fusion, pred[16]{0:T(512)(128)(4,1)S(1)} %dynamic-slice_reduce_fusion.1), kind=kOutput, calls=%fused_computation.4 | convolution fusion | flops 12976192 | bytes 7077968 | tf_op jit(solution)/shard_map/dot_general | solution.py:98
  (40 shorter events, 15.0 us)
Async XLA Ops:
  7.2 232.0 %all-gather.5.cloned.1.call-start = ((), (), s32[]{:S(2)}) async-start(), calls=%async_computation.2 | async-start | bytes 56623104 | tf_op jit(solution)/shard_map/all_gather | solution.py:22
  7.9 342.0 %all-gather.9.cloned.1.call-start = ((), (), s32[]{:S(2)}) async-start(), calls=%async_computation.5 | async-start | bytes 13369344 | tf_op jit(solution)/shard_map/all_gather | solution.py:45
  259.1 3.5 copy-start.2
  259.1 3.5 copy-start.3
  259.2 4.0 copy-start.1
  261.9 161.2 %all-gather.7.cloned.1.call-start = ((), (), s32[]{:S(2)}) async-start(), calls=%async_computation.4 | async-start | bytes 9437184 | tf_op jit(solution)/shard_map/all_gather | solution.py:71
  262.6 434.3 %reduce-scatter.2.cloned.1.call-start = ((), (), s32[]{:S(2)}) async-start(), calls=%async_computation.3 | async-start | bytes 9437184 | tf_op jit(solution)/shard_map/reduce_scatter | solution.py:67
  381.5 13.7 %copy-start = (bf16[8,64,6,128]{3,2,1,0:T(8,128)(2,1)S(1)}, bf16[8,64,6,128]{3,2,1,0:T(8,128)(2,1)}, u32[]{:S(2)}) copy-start(bf16[8,64,6,128]{3,2,1,0:T(8,128)(2,1)} %reshape.57) | copy-start | bytes 2359300
  552.7 115.4 %all-to-all-start = ((bf16[16,2,98304]{2,1,0:T(2,128)(2,1)}), bf16[16,2,98304]{2,1,0:T(2,128)(2,1)}, u32[]{:S(2)}, u32[]{:S(2)}) async-start(bf16[16,2,98304]{2,1,0:T(2,128)(2,1)} %reshape.67), calls=%async_computation.1 | async-start | bytes 12582912 | tf_op jit(solution)/shard_map/all_to_all | solution.py:97
Sparse Core Ops, SparseCore 0:
  9.7 229.4 all-gather.4
  262.0 87.8 all-gather.8
  351.6 51.1 all-gather.6
  423.2 53.9 reduce-scatter.1
